TPU v7x, 32 devices: a whole 2x2x4 slice. The times are simulated.
32 devices in a mesh: grp: 8 (over z, x), sub: 4 (over y, core).
Axes of the slice: x: 2, y: 2, z: 4, core: 2. Of those that a mesh axis runs over, the one named last changes fastest.
Arguments:
- ham_columns: bfloat16 [96, 5, 128, 128], P(('grp', 'sub')), may hold values from -2.2 to 2.2, as said below
- bond_mask: int32 [96, 4], P(('grp', 'sub')), may hold values 0 or 1
- owned_counts: int32 [8, 4], replicated, may hold values from 1 to 3, as said below
- fermi_level: float32 [1], replicated, may hold values from -0.5 to 0.5
Outputs:
- density: bfloat16 [96, 9, 128, 128], P(('grp', 'sub'))
Inputs may be any that keep to these rules, and one draw needn't show every extreme that they name: `ham_columns`: block 0 of every stored block column is symmetric. `bond_mask`: bond lists of slots that hold no cluster are never read. `owned_counts`: along sub, the devices 2k and 2k + 1 of a group own 2 * 2 block columns together, so group g owns clusters g * 8 to (g + 1) * 8 - 1, handed to its devices in order along sub in consecutive runs; no device owns exactly 2; every row has a device that owns 3.
All inputs are finite; a program needn't handle non-finite values. No bound on the sum of `bond_mask` on one device may be relied on, other than what follows from the above.
Results may differ from a plain program's by a relative error of at most 0.0025.
Values may be sent and summed in bfloat16 or wider, within the bound.
A program may use at most 64 MiB of HBM per device.

v0:
```python
import jax
import jax.numpy as jnp
from jax import lax
from jax.sharding import PartitionSpec as P

COLS_MEAN = 2


spectral_span = 4.0


def extended(array, sides, width):
    for axis, dim in sides:
        size, length = (lax.axis_size(axis), array.shape[dim])
        up = [(i, (i + 1) % size) for i in range(size)]
        down = [(j, i) for i, j in up]
        last = lax.slice_in_dim(array, length - width, length, axis=dim)
        leading = lax.slice_in_dim(array, 0, width, axis=dim)
        before = lax.ppermute(last, axis, up)
        after = lax.ppermute(leading, axis, down)
        array = jnp.concatenate([before, array, after], axis=dim)
    return array


def partner(value, axis, distance):
    mask = 2**distance
    pairs = [(source, source ^ mask) for source in range(lax.axis_size(axis))]
    return lax.ppermute(value, axis, pairs)


def build_tile(window_cols, window_bonds, chemical):
    reach_len = window_bonds.shape[1]
    window_len = window_cols.shape[0]
    block_width = window_cols.shape[2]
    identity = jnp.eye(block_width, dtype=jnp.float32)
    bond_values = window_bonds.astype(jnp.float32)
    living = []
    for member in range(window_len):
        if member == reach_len:
            living.append(jnp.ones((), jnp.float32))
        elif member > reach_len:
            living.append(bond_values[reach_len, member - reach_len - 1])
        else:
            living.append(bond_values[member, reach_len - member - 1])
    rows_list = []
    for row_blk in range(window_len):
        pieces = []
        for col_blk in range(window_len):
            distance = row_blk - col_blk
            weight = living[row_blk] * living[col_blk]
            if distance == 0:
                block_value = (
                    window_cols[row_blk, 0].astype(jnp.float32) - chemical * identity
                ) * weight
            elif 0 < distance <= reach_len:
                block_value = window_cols[col_blk, distance].astype(jnp.float32) * (
                    weight * bond_values[col_blk, distance - 1]
                )
            elif 0 < -distance <= reach_len:
                block_value = window_cols[row_blk, -distance].astype(jnp.float32).T * (
                    weight * bond_values[row_blk, -distance - 1]
                )
            else:
                block_value = jnp.zeros((block_width, block_width), jnp.float32)
            pieces.append(block_value)
        rows_list.append(jnp.concatenate(pieces, axis=1))
    return (jnp.concatenate(rows_list, axis=0) / spectral_span).astype(jnp.bfloat16)


def product(matrix, vector):
    return jnp.dot(matrix, vector.astype(jnp.bfloat16), preferred_element_type=jnp.float32)


def apply_rest(matrix, first_term):
    second = product(matrix, first_term)
    third_term = product(matrix, second)
    return 1.5 * first_term - 0.5 * third_term


def density_column(matrix, window_len, block_width):
    center = (window_len - 1) // 2
    first_term = matrix[:, center * block_width : (center + 1) * block_width].astype(jnp.float32)
    step_one = apply_rest(matrix, first_term)
    step_two = apply_rest(matrix, product(matrix, step_one))
    step_three = apply_rest(matrix, product(matrix, step_two))
    sign_column = 1.5 * step_one - 0.5 * step_three
    above = jnp.zeros((center * block_width, block_width), jnp.float32)
    selector = jnp.concatenate([above, jnp.eye(block_width, dtype=jnp.float32), above], axis=0)
    result = (0.5 * (selector - sign_column)).astype(jnp.bfloat16)
    return result.reshape(window_len, block_width, block_width)


def window_result(run_cols, run_bonds, first_row, chemical):
    window_len = 2 * run_bonds.shape[1] + 1
    block_width = run_cols.shape[2]
    window_cols = lax.dynamic_slice_in_dim(run_cols, first_row, window_len, 0)
    window_bonds = lax.dynamic_slice_in_dim(run_bonds, first_row, window_len, 0)
    matrix = build_tile(window_cols, window_bonds, chemical)
    return density_column(matrix, window_len, block_width)


def body(ham_columns, bond_mask, owned_counts, fermi_level):
    reach_len = bond_mask.shape[1]
    slots_here = ham_columns.shape[0]
    group_size = lax.axis_size("sub")
    chemical = fermi_level[0]
    counts_flat = owned_counts.reshape(-1)
    group_index = lax.axis_index("grp")
    member_index = lax.axis_index("sub")
    device_index = group_index * group_size + member_index
    my_count = counts_flat[device_index]
    slot_range = jnp.arange(slots_here, dtype=jnp.int32)
    in_use = slot_range < my_count
    gathered_cols, gathered_bonds = (
        lax.all_gather(ham_columns, "sub", axis=0, tiled=True),
        lax.all_gather(bond_mask, "sub", axis=0, tiled=True),
    )
    group_counts = lax.dynamic_index_in_dim(owned_counts, group_index, 0, keepdims=False)
    group_ends = jnp.cumsum(group_counts)
    group_starts = group_ends - group_counts
    group_cols = COLS_MEAN * group_size
    positions = jnp.arange(group_cols, dtype=jnp.int32)
    owner_index = jnp.sum((group_ends[None, :] <= positions[:, None]).astype(jnp.int32), axis=1)
    gather_index = owner_index * slots_here + positions - group_starts[owner_index]
    local_cols = jnp.take(gathered_cols, gather_index, axis=0)
    local_bonds = jnp.take(gathered_bonds, gather_index, axis=0)
    edge_cols, edge_bonds = (
        extended(local_cols, (("grp", 0),), reach_len),
        extended(local_bonds, (("grp", 0),), reach_len),
    )
    first_rows = member_index * COLS_MEAN + jnp.arange(COLS_MEAN, dtype=jnp.int32)
    results = lax.map(
        lambda first_row: window_result(edge_cols, edge_bonds, first_row, chemical), first_rows
    )
    partner_results = partner(results, "sub", 0)
    is_odd = member_index % 2
    lower_first = jnp.concatenate([results, partner_results], axis=0)
    upper_first = jnp.concatenate([partner_results, results], axis=0)
    pair_results = jnp.where(is_odd == 0, lower_first, upper_first)
    pair_start = (member_index - is_odd) * COLS_MEAN
    wanted = jnp.minimum(group_starts[member_index] - pair_start + slot_range, 2 * COLS_MEAN - 1)
    picked = jnp.take(pair_results, wanted, axis=0)
    return jnp.where(in_use[:, None, None, None], picked, jnp.zeros_like(picked))


def solution(mesh):
    placed = (P(("grp", "sub"), None, None, None), P(("grp", "sub"), None), P(), P())
    return jax.shard_map(
        body,
        mesh=mesh,
        in_specs=placed,
        out_specs=P(("grp", "sub"), None, None, None),
        check_vma=False,
    )
```

profile of v0, /device:TPU:0, one launch (start us, length us, event | category | flops | bytes accessed | tf_op | source)
XLA Modules:
  0.0 352.6 jit_solution(4052440390558888553)
XLA Ops:
  8.3 6.4 %all-gather = s32[4,3,4]{2,1,0:T(4,128)S(1)} all-gather(s32[1,3,4]{2,1,0:T(4,128)} %bitcast.405), channel_id=1, replica_groups=mesh['grp'=8,'sub'=4] {'sub'}, dimensions={0}, use_global_device_ids=true | all-gather | bytes 240 | tf_op jit(solution)/shard_map/all_gather | solution.py:116
  16.0 17.5 %all-gather.3.cloned.1.call-done = bf16[12,5,128,128]{3,2,1,0:T(8,128)(2,1)} async-done(((bf16[3,5,128,128]{3,2,1,0:T(8,128)(2,1)}), bf16[12,5,128,128]{3,2,1,0:T(8,128)(2,1)}) %all-gather.3.cloned.1.call-update) | async-done | bytes 1966096 | tf_op jit(solution)/shard_map/all_gather | solution.py:115
  33.5 2.3 gather_fusion.1
  37.0 4.2 %collective-permute-start.1 = (bf16[4,5,128,128]{3,2,1,0:T(8,128)(2,1)}, bf16[4,5,128,128]{3,2,1,0:T(8,128)(2,1)S(1)}, u32[]{:S(2)}, u32[]{:S(2)}) collective-permute-start(bf16[4,5,128,128]{3,2,1,0:T(8,128)(2,1)} %get-tuple-element.119), channel_id=1, source_target_pairs={{4,0},{8,4},{12,8},{16,12},{20,16},{24,20},{28,24},{0,28},{5,1},{9... | collective-permute-start | bytes 1966088 | tf_op jit(solution)/shard_map/ppermute | solution.py:20
  41.3 4.7 %collective-permute-start.3 = (s32[4,4]{1,0:T(4,128)S(1)}, s32[4,4]{1,0:T(4,128)S(1)}, u32[]{:S(2)}, u32[]{:S(2)}) collective-permute-start(s32[4,4]{1,0:T(4,128)S(1)} %get-tuple-element.121), channel_id=1, source_target_pairs={{4,0},{8,4},{12,8},{16,12},{20,16},{24,20},{28,24},{0,28},{5,1},{9... | collective-permute-start | bytes 200 | tf_op jit(solution)/shard_map/ppermute | solution.py:20
  46.1 22.1 %collective-permute-done.3 = s32[4,4]{1,0:T(4,128)S(1)} collective-permute-done((s32[4,4]{1,0:T(4,128)S(1)}, s32[4,4]{1,0:T(4,128)S(1)}, u32[]{:S(2)}, u32[]{:S(2)}) %collective-permute-start.3) | collective-permute-done | bytes 96 | tf_op jit(solution)/shard_map/ppermute | solution.py:20
  70.2 269.5 %while.10 = (s32[]{:T(128)}, bf16[2,9,128,128]{3,2,1,0:T(8,128)(2,1)}, s32[2]{0:T(128)S(1)}, bf16[16,5,128,128]{3,2,1,0:T(8,128)(2,1)}, f32[]{:T(128)}, /*index=...) while((s32[]{:T(128)}, ...), condition=%wide.region_3.4_spmd, body=%wide.region_2.3_spmd.sunk | while | flops 2726674432 | bytes 48746780 | solution.py:132
  74.7 2.1 constant_dynamic-update-slice_fusion.81
  151.5 2.1 fusion.122
  176.7 2.1 fusion.126
  185.2 2.1 fusion.128
  187.3 2.9 multiply_convert_fusion.2
  190.8 3.3 fusion.130
  196.9 3.3 fusion.132
  200.2 3.9 %fusion.133 = bf16[1152,128]{1,0:T(8,128)(2,1)S(1)} fusion(bf16[1152,1152]{1,0:T(8,128)(2,1)S(1)} %multiply_convert_fusion.2, f32[512,128]{1,0:T(8,128)S(1)} %broadcast.398, f32[128,128]{1,0:T(8,128)} %fusion.129, f32[1152,128]{1,0:T(8,128)} %fusion.132, f32[1152,128]{1,0:T(8,128)} %fusion.130), kind=kOutput, calls=%fused_computation.16.clone.1 | convolution fusion | flops 681394176 | bytes 4456448 | tf_op jit(solution)/shard_map/while/body/eval_jaxpr/dot_general | solution.py:71
  209.4 2.1 constant_dynamic-update-slice_fusion.81
  286.2 2.1 fusion.122
  301.7 2.1 fusion.124
  311.5 2.1 fusion.126
  320.0 2.1 fusion.128
  322.0 2.9 multiply_convert_fusion.2
  325.6 3.3 fusion.130
  331.7 3.3 fusion.132
  335.0 3.9 %fusion.133 = bf16[1152,128]{1,0:T(8,128)(2,1)S(1)} fusion(bf16[1152,1152]{1,0:T(8,128)(2,1)S(1)} %multiply_convert_fusion.2, f32[512,128]{1,0:T(8,128)S(1)} %broadcast.398, f32[128,128]{1,0:T(8,128)} %fusion.129, f32[1152,128]{1,0:T(8,128)} %fusion.132, f32[1152,128]{1,0:T(8,128)} %fusion.130), kind=kOutput, calls=%fused_computation.16.clone.1 | convolution fusion | flops 681394176 | bytes 4456448 | tf_op jit(solution)/shard_map/while/body/eval_jaxpr/dot_general | solution.py:71
  (261 shorter events, 144.4 us)
Async XLA Ops:
  6.5 26.9 %all-gather.3.cloned.1.call-start = ((), (), s32[]{:S(2)}) async-start(), calls=%async_computation | async-start | bytes 2457600 | tf_op jit(solution)/shard_map/all_gather | solution.py:115
  37.0 31.5 %collective-permute-start.1 = (bf16[4,5,128,128]{3,2,1,0:T(8,128)(2,1)}, bf16[4,5,128,128]{3,2,1,0:T(8,128)(2,1)S(1)}, u32[]{:S(2)}, u32[]{:S(2)}) collective-permute-start(bf16[4,5,128,128]{3,2,1,0:T(8,128)(2,1)} %get-tuple-element.119), channel_id=1, source_target_pairs={{4,0},{8,4},{12,8},{16,12},{20,16},{24,20},{28,24},{0,28},{5,1},{9... | collective-permute-start | bytes 1966088 | tf_op jit(solution)/shard_map/ppermute | solution.py:20
  41.2 27.2 %collective-permute-start = (bf16[4,5,128,128]{3,2,1,0:T(8,128)(2,1)S(1)}, bf16[4,5,128,128]{3,2,1,0:T(8,128)(2,1)S(1)}, u32[]{:S(2)}, u32[]{:S(2)}) collective-permute-start(bf16[4,5,128,128]{3,2,1,0:T(8,128)(2,1)S(1)} %get-tuple-element.118), channel_id=1, source_target_pairs={{0,4},{4,8},{8,12},{12,16},{16,20},{20,24},{24,28},{28,0},{1,5},{5... | collective-permute-start | bytes 1966088 | tf_op jit(solution)/shard_map/ppermute | solution.py:19
  41.3 26.9 %collective-permute-start.3 = (s32[4,4]{1,0:T(4,128)S(1)}, s32[4,4]{1,0:T(4,128)S(1)}, u32[]{:S(2)}, u32[]{:S(2)}) collective-permute-start(s32[4,4]{1,0:T(4,128)S(1)} %get-tuple-element.121), channel_id=1, source_target_pairs={{4,0},{8,4},{12,8},{16,12},{20,16},{24,20},{28,24},{0,28},{5,1},{9... | collective-permute-start | bytes 200 | tf_op jit(solution)/shard_map/ppermute | solution.py:20
  46.0 22.3 %collective-permute-start.2 = (s32[4,4]{1,0:T(4,128)S(1)}, s32[4,4]{1,0:T(4,128)S(1)}, u32[]{:S(2)}, u32[]{:S(2)}) collective-permute-start(s32[4,4]{1,0:T(4,128)S(1)} %get-tuple-element.120), channel_id=1, source_target_pairs={{0,4},{4,8},{8,12},{12,16},{16,20},{20,24},{24,28},{28,0},{1,5},{5... | collective-permute-start | bytes 200 | tf_op jit(solution)/shard_map/ppermute | solution.py:19
  70.2 269.5 %copy-start = (s32[8,4]{0,1:T(4,128)S(1)}, s32[8,4]{0,1:T(4,128)}, u32[]{:S(2)}) copy-start(s32[8,4]{0,1:T(4,128)} %param.8) | copy-start | bytes 388
  339.7 2.7 collective-permute-start.4
Sparse Core Ops, SparseCore 0:
  8.9 24.5 all-gather.2
where the time goes:
time: 359 us; the launch traced here: 353 us
  other arithmetic  112 us (31%)
  loops' own time  91.3 us (25%)
  local copies, waits for them, and re-layouts  52.4 us (15%)
  waiting for transfers between devices  40.3 us (11%)
  matrix products  26.7 us (7%)
  between operations  14.1 us (4%)
  starting transfers between devices  8.96 us (2%)
  blocking collectives  6.35 us (2%)
    another operation x1, loops' own time, body(): lax.map(lambda first_row: window_result(edge_cols, edge_bonds, first_row,...  91.3 us
    while x84, other arithmetic  90.3 us
    while x72, local copies, waits for them, and re-layouts  33.7 us
    dot_general x10, matrix products, product(): jnp.dot(matrix, vector.astype(jnp.bfloat16), preferred_element_type=jnp.f...  26.7 us
    ppermute x2, waiting for transfers between devices, extended(): after = lax.ppermute(leading, axis, down)  22.1 us
    all_gather x1, waiting for transfers between devices, body(): lax.all_gather(ham_columns, 'sub', axis=0, tiled=True)  17.5 us
    ppermute x2, starting transfers between devices, extended(): after = lax.ppermute(leading, axis, down)  8.95 us
  transfers between devices with their start and end apart: 6, of which 2 were waited for; matrix products, arithmetic and copies ran while one was open for 1% of the time, Pallas kernels for 0%

commit v1 on v0

v1 whole, which is shorter than its diff:
```python
import functools

import jax
import jax.numpy as jnp
from jax import lax
from jax.experimental import pallas as pl
from jax.experimental.pallas import tpu as pltpu
from jax.sharding import PartitionSpec as P

MESH = pl.DeviceIdType.MESH
SPAN = 4.0
PAD = 16


def kernel(sizes, ham, bonds, counts, fermi, results, swapped_result,
           win, raw, raw_bonds, band, mask, first, kept, vec_a, vec_b,
           swap_send, swap_recv, out_send, out_recv, send_sem, recv_sem):
    n_grp, n_sub, reach, bs = sizes
    n_win = 2 * reach + 2
    total = n_grp * n_sub
    grp, sub = lax.axis_index("grp"), lax.axis_index("sub")
    me = grp * n_sub + sub
    odd = lax.rem(sub, 2)
    rows = (reach + 1) * bs

    def place(d):
        d = lax.rem(d + total, total)
        return (lax.div(d, n_sub), lax.rem(d, n_sub))

    partner = (grp, sub + 1 - 2 * odd)

    barrier = pltpu.get_barrier_semaphore()
    for shift in (-2, -1, 1, 2):
        pl.semaphore_signal(barrier, inc=1, device_id=place(me + shift), device_id_type=MESH)
    pl.semaphore_wait(barrier, 4)

    slot = 2 - 2 * odd
    swaps = []
    for i, (src, dst) in enumerate(((ham.at[slot], raw), (bonds.at[slot], raw_bonds))):
        swap = pltpu.make_async_remote_copy(
            src_ref=src, dst_ref=dst, send_sem=swap_send.at[i], recv_sem=swap_recv.at[i],
            device_id=partner, device_id_type=MESH)
        swap.start()
        swaps.append(swap)

    mine = counts[grp, sub]
    long_one = (mine > 2).astype(jnp.float32)
    odd_f = odd.astype(jnp.float32)
    c0_slot0 = 1.0 - odd_f
    c0_slot1 = odd_f * long_one
    c0_swap = odd_f * (1.0 - long_one)
    c1_slot1 = (1.0 - odd_f) * long_one
    c1_swap = (1.0 - odd_f) * (1.0 - long_one)
    c1_slot2 = odd_f * long_one
    c1_slot0 = odd_f * (1.0 - long_one)
    chemical = fermi[0]

    eye = (lax.broadcasted_iota(jnp.int32, (bs, bs), 0)
           == lax.broadcasted_iota(jnp.int32, (bs, bs), 1)).astype(jnp.float32)
    for swap in swaps:
        swap.wait()

    zero = jnp.zeros((2 * bs, 2 * bs), jnp.bfloat16)

    def fill(col, sources):
        w = reach + col
        bond = sum(b[...].astype(jnp.float32) * k for b, _, k in sources)
        win[w, rows:rows + PAD, :] = bond.astype(jnp.bfloat16)
        for o in range(reach + 1):
            block = sum(h[o].astype(jnp.float32) * (k * (1.0 / SPAN)) for _, h, k in sources)
            if o == 0:
                block = block - (chemical * (1.0 / SPAN)) * eye
            else:
                block = block * bond[o - 1:o, :]
            win[w, o * bs:(o + 1) * bs, :] = block.astype(jnp.bfloat16)

    fill(0, ((bonds.at[0], ham.at[0], c0_slot0), (bonds.at[1], ham.at[1], c0_slot1),
             (raw_bonds, raw, c0_swap)))
    fill(1, ((bonds.at[0], ham.at[0], c1_slot0), (bonds.at[1], ham.at[1], c1_slot1),
             (bonds.at[2], ham.at[2], c1_slot2), (raw_bonds, raw, c1_swap)))

    plan = []
    c = reach
    plan.append((1, win.at[pl.ds(c, 2)], win.at[pl.ds(c - 2, 2)]))
    plan.append((2, win.at[pl.ds(c, 2)], win.at[pl.ds(c - 4, 2)]))
    for shift in (-1, -2):
        for col in range(2):
            w = c + col - 2 * shift
            part = pl.ds(0, min(reach + 1, n_win - w) * bs)
            plan.append((shift, win.at[c + col, part], win.at[w, part]))
    copies = []
    for i, (shift, src, dst) in enumerate(plan):
        copy = pltpu.make_async_remote_copy(
            src_ref=src, dst_ref=dst, send_sem=send_sem.at[i], recv_sem=recv_sem.at[i],
            device_id=place(me + shift), device_id_type=MESH)
        copy.start()
        copies.append(copy)

    def build(w):
        for o in range(min(reach + 1, n_win - w)):
            block = win[w, o * bs:(o + 1) * bs, :]
            band[(w + o) * bs:(w + o + 1) * bs, w * bs:(w + 1) * bs] = block
            if o:
                band[w * bs:(w + 1) * bs, (w + o) * bs:(w + o + 1) * bs] = block.T

    for w in range(0, n_win - reach - 1, 2):
        v = w + reach + 1
        band[w * bs:(w + 1) * bs, v * bs:(v + 1) * bs] = zero[:bs, :bs]
        band[v * bs:(v + 1) * bs, w * bs:(w + 1) * bs] = zero[:bs, :bs]
    build(c)
    build(c + 1)
    for i, columns in ((0, (c - 2, c - 1)), (2, (c + 2,)), (3, (c + 3,)),
                       (4, (c + 4,)), (5, (c + 5,)), (1, (c - 4, c - 3))):
        copies[i].wait_recv()
        for w in columns:
            build(w)

    one = jnp.ones((1, bs), jnp.float32)
    nil = jnp.zeros((1, bs), jnp.float32)

    def live(center, w):
        distance = abs(w - center)
        if distance == 0:
            return one
        if distance > reach:
            return nil
        tile = win[min(w, center), rows:rows + PAD, :].astype(jnp.float32)
        return tile[distance - 1:distance, :]

    for w in range(n_win):
        mask[w:w + 1, 0:bs] = live(c, w)
        mask[w:w + 1, bs:2 * bs] = live(c + 1, w)

    pairs = n_win // 2

    def masked(r, value):
        top = value[:bs] * mask[2 * r:2 * r + 1, :]
        low = value[bs:] * mask[2 * r + 1:2 * r + 2, :]
        return jnp.concatenate([top, low], axis=0)

    def product(source, r):
        lo = max(0, 2 * r - reach) * bs
        hi = min(n_win, 2 * r + reach + 2) * bs
        value = jnp.dot(band[2 * r * bs:(2 * r + 2) * bs, lo:hi], source[lo:hi, :],
                        preferred_element_type=jnp.float32)
        return masked(r, value)

    def at(r):
        return slice(2 * r * bs, (2 * r + 2) * bs)

    for r in range(pairs):
        value = masked(r, band[at(r), c * bs:(c + 2) * bs].astype(jnp.float32))
        first[at(r), :] = value
        vec_a[at(r), :] = value.astype(jnp.bfloat16)

    for r in range(pairs):
        vec_b[at(r), :] = product(vec_a, r).astype(jnp.bfloat16)
    for r in range(pairs):
        step = 1.5 * first[at(r), :] - 0.5 * product(vec_b, r)
        kept[at(r), :] = step
        vec_a[at(r), :] = step.astype(jnp.bfloat16)

    for r in range(pairs):
        value = product(vec_a, r)
        first[at(r), :] = value
        vec_b[at(r), :] = value.astype(jnp.bfloat16)
    for r in range(pairs):
        vec_a[at(r), :] = product(vec_b, r).astype(jnp.bfloat16)
    for r in range(pairs):
        step = 1.5 * first[at(r), :] - 0.5 * product(vec_a, r)
        vec_b[at(r), :] = step.astype(jnp.bfloat16)

    for r in range(pairs):
        value = product(vec_b, r)
        first[at(r), :] = value
        vec_a[at(r), :] = value.astype(jnp.bfloat16)
    for r in range(pairs):
        vec_b[at(r), :] = product(vec_a, r).astype(jnp.bfloat16)
    for r in range(pairs):
        step = 1.5 * first[at(r), :] - 0.5 * product(vec_b, r)
        sign = 1.5 * kept[at(r), :] - 0.5 * step
        for half in range(2):
            w = 2 * r + half
            for k in range(2):
                if not 0 <= w - k <= 2 * reach:
                    continue
                value = -0.5 * sign[half * bs:(half + 1) * bs, k * bs:(k + 1) * bs]
                if w == c + k:
                    value = 0.5 * eye + value
                results[k, w - k] = value.astype(jnp.bfloat16)

    swap = pltpu.make_async_remote_copy(
        src_ref=results.at[1 - odd], dst_ref=swapped_result,
        send_sem=out_send, recv_sem=out_recv, device_id=partner, device_id_type=MESH)
    swap.start()
    for copy in copies:
        copy.wait_send()
    swap.wait()


def body(n_grp, n_sub, ham_columns, bond_mask, owned_counts, fermi_level):
    slots, depth, bs, _ = ham_columns.shape
    reach = depth - 1
    n_win = 2 * reach + 2
    vmem, smem = pltpu.VMEM, pltpu.SMEM
    wide = jnp.pad(bond_mask.astype(jnp.bfloat16), ((0, 0), (0, PAD - reach)))
    wide = jnp.broadcast_to(wide[:, :, None], (slots, PAD, bs))
    sizes = (n_grp, n_sub, reach, bs)
    results, swapped = pl.pallas_call(
        functools.partial(kernel, sizes),
        out_shape=(
            jax.ShapeDtypeStruct((2, 2 * reach + 1, bs, bs), jnp.bfloat16),
            jax.ShapeDtypeStruct((2 * reach + 1, bs, bs), jnp.bfloat16),
        ),
        in_specs=[
            pl.BlockSpec(memory_space=vmem), pl.BlockSpec(memory_space=vmem),
            pl.BlockSpec(memory_space=smem), pl.BlockSpec(memory_space=smem),
        ],
        out_specs=(pl.BlockSpec(memory_space=vmem), pl.BlockSpec(memory_space=vmem)),
        scratch_shapes=[
            vmem((n_win, depth * bs + PAD, bs), jnp.bfloat16),
            vmem((depth, bs, bs), jnp.bfloat16),
            vmem((PAD, bs), jnp.bfloat16),
            vmem((n_win * bs, n_win * bs), jnp.bfloat16),
            vmem((16, 2 * bs), jnp.float32),
            vmem((n_win * bs, 2 * bs), jnp.float32),
            vmem((n_win * bs, 2 * bs), jnp.float32),
            vmem((n_win * bs, 2 * bs), jnp.bfloat16),
            vmem((n_win * bs, 2 * bs), jnp.bfloat16),
            pltpu.SemaphoreType.DMA((2,)),
            pltpu.SemaphoreType.DMA((2,)),
            pltpu.SemaphoreType.DMA,
            pltpu.SemaphoreType.DMA,
            pltpu.SemaphoreType.DMA((6,)),
            pltpu.SemaphoreType.DMA((6,)),
        ],
        compiler_params=pltpu.CompilerParams(collective_id=0, has_side_effects=True),
    )(ham_columns, wide, owned_counts, fermi_level)

    grp, sub = lax.axis_index("grp"), lax.axis_index("sub")
    odd = (sub % 2) == 1
    long_one = owned_counts[grp, sub] > 2
    none = jnp.zeros_like(swapped)
    slot0 = jnp.where(odd, jnp.where(long_one, swapped, results[1]), results[0])
    slot1 = jnp.where(long_one, jnp.where(odd, results[0], results[1]), none)
    slot2 = jnp.where(long_one, jnp.where(odd, results[1], swapped), none)
    return jnp.stack([slot0, slot1, slot2])


def solution(mesh):
    n_grp, n_sub = mesh.shape["grp"], mesh.shape["sub"]
    placed = (P(("grp", "sub"), None, None, None), P(("grp", "sub"), None), P(), P())
    return jax.shard_map(
        functools.partial(body, n_grp, n_sub),
        mesh=mesh,
        in_specs=placed,
        out_specs=P(("grp", "sub"), None, None, None),
        check_vma=False,
    )
```

time: 359 us -> 37.8 us (0.11); the launches traced: 353 us -> 37.6 us
  other arithmetic: 112 us -> 2.3 us
  loops' own time: 91.3 us -> 0 us
  local copies, waits for them, and re-layouts: 52.4 us -> 2.69 us
  waiting for transfers between devices: 40.3 us -> 0 us
  Pallas kernels: 0 us -> 31.3 us
  matrix products: 26.7 us -> 0 us
  between operations: 14.1 us -> 1.36 us
  starting transfers between devices: 8.96 us -> 0 us
  blocking collectives: 6.35 us -> 0 us
    another operation x1 -> x0, loops' own time: 91.3 us -> none  [body(): lax.map(lambda first_row: window_result(edge_cols, edge_bonds, first_row,...]
    while x84 -> x0, other arithmetic: 90.3 us -> none
    while x72 -> x0, local copies, waits for them, and re-layouts: 33.7 us -> none
    pallas_call x0 -> x1, Pallas kernels: none -> 31.3 us  [body(): pl.pallas_call(functools.partial(kernel, sizes), out_shape=(jax.ShapeDtyp...]
    dot_general x10 -> x0, matrix products: 26.7 us -> none  [product(): jnp.dot(matrix, vector.astype(jnp.bfloat16), preferred_element_type=jnp.f...]
    ppermute x5 -> x0, waiting for transfers between devices: 22.1 us -> none  [the longest x2 22.1 us: extended(): after = lax.ppermute(leading, axis, down)]
    all_gather x1 -> x0, waiting for transfers between devices: 17.5 us -> none  [body(): lax.all_gather(ham_columns, 'sub', axis=0, tiled=True)]
    ppermute x5 -> x0, starting transfers between devices: 8.96 us -> none  [the longest x2 8.95 us: extended(): after = lax.ppermute(leading, axis, down)]
  transfers between devices with their start and end apart: 6 -> 0, of which waited for: 2 -> 0; matrix products, arithmetic and copies ran while one was open for 1% -> 0% of each run, Pallas kernels for 0% -> 0%
where the time goes in v1:
time: 37.8 us; the launch traced here: 37.6 us
  Pallas kernels  31.3 us (83%)
  local copies, waits for them, and re-layouts  2.69 us (7%)
  other arithmetic  2.3 us (6%)
  between operations  1.36 us (4%)
    pallas_call x1, Pallas kernels, body(): pl.pallas_call(functools.partial(kernel, sizes), out_shape=(jax.ShapeDtyp...  31.3 us
    another operation x2, other arithmetic, body(): return jnp.stack([slot0, slot1, slot2])  2.27 us
    unnamed x7, local copies, waits for them, and re-layouts  1.42 us

profile of v1, /device:TPU:0, one launch (start us, length us, event | category | flops | bytes accessed | tf_op | source)
XLA Modules:
  0.0 37.6 jit_solution(16926177718451745616)
XLA Ops:
  0.0 0.0 copy-start.1
  0.0 0.7 %copy-done.1 = s32[8,4]{0,1:T(4,128)S(1)} copy-done((s32[8,4]{0,1:T(4,128)S(1)}, s32[8,4]{0,1:T(4,128)}, u32[]{:S(2)}) %copy-start.1) | copy-done | bytes 152
  0.7 0.6 %dynamic_slice.3 = s32[1,1]{0,1:T(1,128)} dynamic-slice(s32[8,4]{0,1:T(4,128)S(1)} %copy-done.1, s32[]{:T(128)S(6)} %select_n.51, s32[]{:T(128)S(6)} %select_n.52), dynamic_slice_sizes={1,1} | dynamic-slice | bytes 12 | tf_op jit(solution)/shard_map/dynamic_slice | solution.py:242
  1.3 0.0 copy-start.2
  1.9 0.0 copy-done.2
  2.0 0.7 %broadcast_in_dim.11.bonds = bf16[3,16,128]{2,1,0:T(8,128)(2,1)} broadcast(bf16[3,16]{1,0:T(4,128)(2,1)S(1)} %pad.4), dimensions={0,1} | broadcast | bytes 12384 | tf_op jit(solution)/shard_map/broadcast_in_dim | solution.py:207
  2.6 0.7 %copy.5.counts = s32[8,4]{1,0:T(8,128)} copy(s32[8,4]{0,1:T(4,128)S(1)} %copy-done.1) | data formatting | bytes 256 | tf_op args[2]
  4.0 31.3 %shard_map.46 = (bf16[2,9,128,128]{3,2,1,0:T(8,128)(2,1)}, bf16[9,128,128]{2,1,0:T(8,128)(2,1)}) custom-call(bf16[3,5,128,128]{3,2,1,0:T(8,128)(2,1)} %ham.1, bf16[3,16,128]{2,1,0:T(8,128)(2,1)} %broadcast_in_dim.11.bonds, s32[8,4]{1,0:T(8,128)} %copy.5.counts, f32[1]{0:T(128)S(6)} %copy.6.fermi), custom_call_target="tpu_custom_call" | custom-call | tf_op jit(solution)/shard_map/pallas_call | solution.py:209
  35.2 0.0 copy-start
  35.2 1.3 %fusion = (bf16[1,9,128,128]{3,2,1,0:T(8,128)(2,1)S(1)}, bf16[1,9,128,128]{3,2,1,0:T(8,128)(2,1)S(1)}) fusion(bf16[9,128,128]{2,1,0:T(8,128)(2,1)} %get-tuple-element.7, pred[]{:T(512)} %bitcast, pred[]{:T(512)S(6)} %eq.5, bf16[2,9,128,128]{3,2,1,0:T(8,128)(2,1)} %get-tuple-element.8), kind=kLoop, calls=%fused_computation.2 | loop fusion | flops 589824 | bytes 1474562 | tf_op jit(solution)/shard_map/stack | solution.py:247
  36.5 0.1 copy-done
  36.6 1.0 %pad_maximum_fusion = bf16[3,9,128,128]{3,2,1,0:T(8,128)(2,1)} fusion(bf16[1,9,128,128]{3,2,1,0:T(8,128)(2,1)S(1)} %get-tuple-element.10, bf16[1,9,128,128]{3,2,1,0:T(8,128)(2,1)S(1)} %select_select_fusion, bf16[1,9,128,128]{3,2,1,0:T(8,128)(2,1)S(1)} %get-tuple-element.9), kind=kLoop, calls=%fused_computation | loop fusion | flops 884736 | bytes 1769472 | tf_op jit(solution)/shard_map/stack | solution.py:247
  (3 shorter events, 0.0 us)
Async XLA Ops:
  0.0 0.7 %copy-start.1 = (s32[8,4]{0,1:T(4,128)S(1)}, s32[8,4]{0,1:T(4,128)}, u32[]{:S(2)}) copy-start(s32[8,4]{0,1:T(4,128)} %param.6) | copy-start | bytes 388
  1.3 0.7 %copy-start.2 = (s32[3,4]{1,0:T(4,128)S(1)}, s32[3,4]{1,0:T(4,128)}, u32[]{:S(2)}) copy-start(s32[3,4]{1,0:T(4,128)} %param.5) | copy-start | bytes 148
  35.2 1.3 %copy-start = (bf16[2,9,128,128]{3,2,1,0:T(8,128)(2,1)S(1)}, bf16[2,9,128,128]{3,2,1,0:T(8,128)(2,1)}, u32[]{:S(2)}) copy-start(bf16[2,9,128,128]{3,2,1,0:T(8,128)(2,1)} %get-tuple-element.8) | copy-start | bytes 1769476

commit v2 on v1

v2 whole, which is shorter than its diff:
```python
import functools

import jax
import jax.numpy as jnp
from jax import lax
from jax.experimental import pallas as pl
from jax.experimental.pallas import tpu as pltpu
from jax.sharding import PartitionSpec as P

MESH = pl.DeviceIdType.MESH
SPAN = 4.0
PAD = 16


def kernel(sizes, ham_hbm, bonds_hbm, counts_hbm, fermi_hbm, out,
           ham, bonds, counts, fermi, win, raw, raw_bonds, band, mask, first, kept,
           vec_a, vec_b, results, swapped_result,
           load_sem, swap_send, swap_recv, out_send, out_recv, send_sem, recv_sem):
    n_grp, n_sub, reach, bs = sizes
    n_win = 2 * reach + 2
    total = n_grp * n_sub
    grp, sub = lax.axis_index("grp"), lax.axis_index("sub")
    me = grp * n_sub + sub
    odd = lax.rem(sub, 2)
    even = 1 - odd
    rows = (reach + 1) * bs
    c = reach

    def place(shift):
        d = lax.rem(me + shift + total, total)
        return (lax.div(d, n_sub), lax.rem(d, n_sub))

    barrier = pltpu.get_barrier_semaphore()
    for shift in (-2, -1, 1, 2):
        pl.semaphore_signal(barrier, inc=1, device_id=place(shift), device_id_type=MESH)

    loads = []
    for i, (src, dst) in enumerate(((counts_hbm, counts), (fermi_hbm, fermi),
                                    (bonds_hbm, bonds), (ham_hbm, ham))):
        load = pltpu.make_async_copy(src, dst, load_sem.at[i])
        load.start()
        loads.append(load)
    zero = jnp.zeros((bs, bs), jnp.bfloat16)
    for w in range(0, n_win - reach - 1, 2):
        v = w + reach + 1
        band[w * bs:(w + 1) * bs, v * bs:(v + 1) * bs] = zero
        band[v * bs:(v + 1) * bs, w * bs:(w + 1) * bs] = zero
    eye = (lax.broadcasted_iota(jnp.int32, (bs, bs), 0)
           == lax.broadcasted_iota(jnp.int32, (bs, bs), 1)).astype(jnp.float32)
    for load in loads:
        load.wait()

    long_one = (counts[grp, sub] > 2).astype(jnp.float32)
    odd_f = odd.astype(jnp.float32)
    chemical = fermi[0]

    def fill(w, sources):
        bond = []
        for o in range(reach):
            lane = sum(b.astype(jnp.float32) * k for b, _, k in sources)
            bond.append(jnp.broadcast_to(lane[:, o:o + 1], (1, bs)))
        tile = jnp.concatenate(bond + [jnp.zeros((PAD - reach, bs), jnp.float32)], axis=0)
        win[w, rows:rows + PAD, :] = tile.astype(jnp.bfloat16)
        for o in range(reach + 1):
            block = sum(h[o].astype(jnp.float32) * (k * (1.0 / SPAN)) for _, h, k in sources)
            if o == 0:
                block = block - (chemical * (1.0 / SPAN)) * eye
            else:
                block = block * bond[o - 1]
            win[w, o * bs:(o + 1) * bs, :] = block.astype(jnp.bfloat16)

    last = odd_f * long_one
    fill(c + odd, ((bonds[0:1, :], ham.at[0], 1.0 - last), (bonds[2:3, :], ham.at[2], last)))

    pl.semaphore_wait(barrier, 4)

    def remote(src, dst, send, recv, device):
        return pltpu.make_async_remote_copy(
            src_ref=src, dst_ref=dst, send_sem=send, recv_sem=recv,
            device_id=device, device_id_type=MESH)

    partner = (grp, sub + 1 - 2 * odd)
    swaps = [remote(ham_hbm.at[2 * even], raw, swap_send.at[0], swap_recv.at[0], partner),
             remote(bonds_hbm, raw_bonds, swap_send.at[1], swap_recv.at[1], partner)]
    for swap in swaps:
        swap.start()

    def part(w):
        if w < c:
            return pl.ds(0, rows + PAD)
        return pl.ds(0, min(reach + 1, n_win - w) * bs)

    def column(i, source, w, shift):
        return remote(win.at[source, part(w)], win.at[w, part(w)],
                      send_sem.at[i], recv_sem.at[w], place(shift))

    def arrive(w):
        column(0, w, w, 1).wait_recv()

    sends_even = ((c, c - 4, 2), (c, c + 2, -1), (c, c - 2, 1))
    sends_odd = ((c + 1, c - 3, 2), (c + 1, c + 5, -2), (c + 1, c + 3, -1))
    later_even = ((c + 1, c - 3, 2), (c + 1, c + 3, -1), (c + 1, c - 1, 1))
    later_odd = ((c, c - 2, 1), (c, c + 4, -2), (c, c + 2, -1))

    @pl.when(odd == 0)
    def _():
        for i, send in enumerate(sends_even):
            column(i, *send).start()

    @pl.when(odd == 1)
    def _():
        for i, send in enumerate(sends_odd):
            column(i, *send).start()

    for swap in swaps:
        swap.wait()
    fill(c + even, ((bonds[1:2, :], ham.at[1], long_one),
                    (jnp.where(odd == 0, raw_bonds[0:1, :], raw_bonds[2:3, :]), raw, 1.0 - long_one)))

    @pl.when(odd == 0)
    def _():
        for i, send in enumerate(later_even):
            column(3 + i, *send).start()

    @pl.when(odd == 1)
    def _():
        for i, send in enumerate(later_odd):
            column(3 + i, *send).start()

    def build(w):
        for o in range(min(reach + 1, n_win - w)):
            block = win[w, o * bs:(o + 1) * bs, :]
            band[(w + o) * bs:(w + o + 1) * bs, w * bs:(w + 1) * bs] = block
            if o:
                band[w * bs:(w + 1) * bs, (w + o) * bs:(w + o + 1) * bs] = block.T

    build(c)
    build(c + 1)

    relay_even = {c - 2: (6, c - 2, c - 4, 1)}
    relay_odd = {c - 3: (6, c - 3, c - 1, -1), c + 2: (7, c + 2, c + 4, -1), c + 3: (8, c + 3, c + 5, -1)}

    @pl.when(odd == 0)
    def _():
        for w in (c + 2, c + 3, c - 4, c - 2, c - 3, c - 1, c + 4, c + 5):
            arrive(w)
            if w in relay_even:
                column(*relay_even[w]).start()
            build(w)

    @pl.when(odd == 1)
    def _():
        for w in (c - 2, c - 1, c - 3, c + 2, c + 3, c + 5, c + 4, c - 4):
            arrive(w)
            if w in relay_odd:
                column(*relay_odd[w]).start()
            build(w)

    one = jnp.ones((1, bs), jnp.float32)
    nil = jnp.zeros((1, bs), jnp.float32)

    def live(center, w):
        distance = abs(w - center)
        if distance == 0:
            return one
        if distance > reach:
            return nil
        tile = win[min(w, center), rows:rows + PAD, :].astype(jnp.float32)
        return tile[distance - 1:distance, :]

    for w in range(n_win):
        mask[w:w + 1, 0:bs] = live(c, w)
        mask[w:w + 1, bs:2 * bs] = live(c + 1, w)

    pairs = n_win // 2

    def give(i):
        span = pl.ds(0, reach + 1) if i == 0 else pl.ds(reach + 1, reach)
        return remote(results.at[even, span], swapped_result.at[span],
                      out_send.at[i], out_recv.at[i], partner)

    def masked(r, value):
        top = value[:bs] * mask[2 * r:2 * r + 1, :]
        low = value[bs:] * mask[2 * r + 1:2 * r + 2, :]
        return jnp.concatenate([top, low], axis=0)

    def product(source, r):
        lo = max(0, 2 * r - reach) * bs
        hi = min(n_win, 2 * r + reach + 2) * bs
        value = jnp.dot(band[2 * r * bs:(2 * r + 2) * bs, lo:hi], source[lo:hi, :],
                        preferred_element_type=jnp.float32)
        return masked(r, value)

    def at(r):
        return slice(2 * r * bs, (2 * r + 2) * bs)

    for r in range(pairs):
        value = masked(r, band[at(r), c * bs:(c + 2) * bs].astype(jnp.float32))
        first[at(r), :] = value
        vec_a[at(r), :] = value.astype(jnp.bfloat16)

    for r in range(pairs):
        vec_b[at(r), :] = product(vec_a, r).astype(jnp.bfloat16)
    for r in range(pairs):
        step = 1.5 * first[at(r), :] - 0.5 * product(vec_b, r)
        kept[at(r), :] = step
        vec_a[at(r), :] = step.astype(jnp.bfloat16)

    for r in range(pairs):
        value = product(vec_a, r)
        first[at(r), :] = value
        vec_b[at(r), :] = value.astype(jnp.bfloat16)
    for r in range(pairs):
        vec_a[at(r), :] = product(vec_b, r).astype(jnp.bfloat16)
    for r in range(pairs):
        step = 1.5 * first[at(r), :] - 0.5 * product(vec_a, r)
        vec_b[at(r), :] = step.astype(jnp.bfloat16)

    for r in range(pairs):
        value = product(vec_b, r)
        first[at(r), :] = value
        vec_a[at(r), :] = value.astype(jnp.bfloat16)
    for r in range(pairs):
        vec_b[at(r), :] = product(vec_a, r).astype(jnp.bfloat16)
    for r in range(pairs):
        step = 1.5 * first[at(r), :] - 0.5 * product(vec_b, r)
        sign = 1.5 * kept[at(r), :] - 0.5 * step
        for half in range(2):
            w = 2 * r + half
            for k in range(2):
                if not 0 <= w - k <= 2 * reach:
                    continue
                value = -0.5 * sign[half * bs:(half + 1) * bs, k * bs:(k + 1) * bs]
                if w == c + k:
                    value = 0.5 * eye + value
                results[k, w - k] = value.astype(jnp.bfloat16)
        if r == reach // 2:
            give(0).start()
    give(1).start()

    even_f, short = 1.0 - odd_f, 1.0 - long_one
    places = ((even_f, odd_f * short, odd_f * long_one),
              (odd_f * long_one, even_f * long_one, None),
              (None, odd_f * long_one, even_f * long_one))

    def write(t, w):
        terms = (results[0, w], results[1, w], swapped_result[w])
        value = sum(k * x.astype(jnp.float32) for k, x in zip(places[t], terms) if k is not None)
        out[t, w] = value.astype(jnp.bfloat16)

    def finish(sends):
        for i, send in enumerate(sends):
            column(i, *send).wait_send()

    @pl.when(odd == 0)
    def _():
        finish(sends_even + later_even + tuple(v[1:] for v in relay_even.values()))

    @pl.when(odd == 1)
    def _():
        finish(sends_odd + later_odd + tuple(v[1:] for v in relay_odd.values()))

    for w in range(2 * reach + 1):
        write(1, w)
    give(0).wait()
    for w in range(reach + 1):
        write(0, w)
        write(2, w)
    give(1).wait()
    for w in range(reach + 1, 2 * reach + 1):
        write(0, w)
        write(2, w)


def body(n_grp, n_sub, ham_columns, bond_mask, owned_counts, fermi_level):
    slots, depth, bs, _ = ham_columns.shape
    reach = depth - 1
    n_win = 2 * reach + 2
    vmem, smem, dma = pltpu.VMEM, pltpu.SMEM, pltpu.SemaphoreType.DMA
    sizes = (n_grp, n_sub, reach, bs)
    return pl.pallas_call(
        functools.partial(kernel, sizes),
        out_shape=jax.ShapeDtypeStruct((slots, 2 * reach + 1, bs, bs), jnp.bfloat16),
        in_specs=[pl.BlockSpec(memory_space=pl.ANY)] * 4,
        out_specs=pl.BlockSpec(memory_space=vmem),
        scratch_shapes=[
            vmem(ham_columns.shape, jnp.bfloat16),
            vmem(bond_mask.shape, jnp.int32),
            smem(owned_counts.shape, jnp.int32),
            smem(fermi_level.shape, jnp.float32),
            vmem((n_win, depth * bs + PAD, bs), jnp.bfloat16),
            vmem((depth, bs, bs), jnp.bfloat16),
            vmem(bond_mask.shape, jnp.int32),
            vmem((n_win * bs, n_win * bs), jnp.bfloat16),
            vmem((16, 2 * bs), jnp.float32),
            vmem((n_win * bs, 2 * bs), jnp.float32),
            vmem((n_win * bs, 2 * bs), jnp.float32),
            vmem((n_win * bs, 2 * bs), jnp.bfloat16),
            vmem((n_win * bs, 2 * bs), jnp.bfloat16),
            vmem((2, 2 * reach + 1, bs, bs), jnp.bfloat16),
            vmem((2 * reach + 1, bs, bs), jnp.bfloat16),
            dma((4,)),
            dma((2,)),
            dma((2,)),
            dma((2,)),
            dma((2,)),
            dma((9,)),
            dma((n_win,)),
        ],
        compiler_params=pltpu.CompilerParams(collective_id=0, has_side_effects=True),
    )(ham_columns, bond_mask, owned_counts, fermi_level)


def solution(mesh):
    n_grp, n_sub = mesh.shape["grp"], mesh.shape["sub"]
    placed = (P(("grp", "sub"), None, None, None), P(("grp", "sub"), None), P(), P())
    return jax.shard_map(
        functools.partial(body, n_grp, n_sub),
        mesh=mesh,
        in_specs=placed,
        out_specs=P(("grp", "sub"), None, None, None),
        check_vma=False,
    )
```

time: 37.8 us -> 29.2 us (0.77)
  Pallas kernels: 31.3 us -> 24.8 us
  other arithmetic: 2.3 us -> 0 us
  local copies, waits for them, and re-layouts: 2.69 us -> 3.52 us
  between operations: 1.36 us -> 0.66 us
    pallas_call x1, Pallas kernels: 31.3 us -> 24.8 us  [body(): pl.pallas_call(functools.partial(kernel, sizes), out_shape=jax.ShapeDtype...]
    another operation x2 -> x0, other arithmetic: 2.27 us -> none  [body(): return jnp.stack([slot0, slot1, slot2])]
    unnamed x7 -> x2, local copies, waits for them, and re-layouts: 1.42 us -> 3.52 us
    broadcast_in_dim x1 -> x0, local copies, waits for them, and re-layouts: 0.67 us -> none  [body(): wide = jnp.broadcast_to(wide[:, :, None], (slots, PAD, bs))]
    dynamic_slice x1 -> x0, local copies, waits for them, and re-layouts: 0.58 us -> none  [body(): long_one = owned_counts[grp, sub] > 2]
where the time goes in v2:
time: 29.2 us; the launch traced here: 29 us
  Pallas kernels  24.8 us (85%)
  local copies, waits for them, and re-layouts  3.52 us (12%)
  between operations  0.66 us (2%)
    pallas_call x1, Pallas kernels, body(): pl.pallas_call(functools.partial(kernel, sizes), out_shape=jax.ShapeDtype...  24.8 us
    unnamed x2, local copies, waits for them, and re-layouts  3.52 us

profile of v2, /device:TPU:0, one launch (start us, length us, event | category | flops | bytes accessed | tf_op | source)
XLA Modules:
  0.0 29.0 jit_solution(44545503168562305)
XLA Ops:
  0.7 1.3 %copy.5.counts_hbm = s32[8,4]{1,0:T(8,128)} copy(s32[8,4]{0,1:T(4,128)} %param.6) | data formatting | bytes 256 | tf_op args[2]
  2.0 24.8 %shard_map.46 = bf16[3,9,128,128]{3,2,1,0:T(8,128)(2,1)} custom-call(bf16[3,5,128,128]{3,2,1,0:T(8,128)(2,1)} %ham_hbm.1, s32[3,4]{1,0:T(4,128)} %bonds_hbm.1, s32[8,4]{1,0:T(8,128)} %copy.5.counts_hbm, f32[1]{0:T(128)S(6)} %copy.7.fermi_hbm), custom_call_target="tpu_custom_call" | custom-call | tf_op jit(solution)/shard_map/pallas_call | solution.py:281
  26.8 2.2 %copy.8 = bf16[3,9,128,128]{3,2,1,0:T(8,128)(2,1)} copy(bf16[3,9,128,128]{3,2,1,0:T(8,128)(2,1)} %shard_map.46) | data formatting | bytes 1769472
